TPU v7x, 32 devices: a whole 2x2x4 slice. The times are simulated.
32 devices in a mesh: aux: 4 (over x, core), orb: 8 (over z, y).
Axes of the slice: x: 2, y: 2, z: 4, core: 2. Of those that a mesh axis runs over, the one named last changes fastest.
Arguments:
- three_center: bfloat16 [640, 8, 3, 4096], P(('aux', 'orb')), may hold values from -1.5 to 1.5
- atom_size: int32 [8], replicated, may hold values from 32 to 64
- tensor_pattern: int32 [40, 8, 3], P('aux', 'orb'), may hold values 0 or 1
- green_occ: bfloat16 [8, 3, 4096], P('orb'), may hold values from -0.5 to 0.5
- green_virt: bfloat16 [8, 3, 4096], P('orb'), may hold values from -0.5 to 0.5
- green_pattern: int32 [8, 3], P('orb'), may hold values 0 or 1
Outputs:
- chi: float32 [640, 640], P(('aux', 'orb'))
Inputs may be any that keep to these rules, and one draw needn't show every extreme that they name: `atom_size`: functions in use per block.
All inputs are finite; a program needn't handle non-finite values. No bound on the sum of `tensor_pattern` or of `green_pattern` on one device may be relied on, other than what follows from the above.
Results may differ from a plain program's by a relative error of at most 0.0041.
Values may be sent and summed in bfloat16 or wider, within the bound.
A program may use at most 128 MiB of HBM per device.

v0:
```python
import jax
import jax.numpy as jnp
from jax import lax
from jax.sharding import PartitionSpec as P

BS = 64
R = 1
W = 3
ABS = 16


def padded(block, sides, width):
    for axis, dim in sides:
        count = lax.axis_size(axis)
        forward = [(i, i + 1) for i in range(count - 1)]
        backward = [(target, source) for source, target in forward]
        low = lax.ppermute(
            lax.slice_in_dim(block, block.shape[dim] - width, None, axis=dim), axis, forward
        )
        high = lax.ppermute(lax.slice_in_dim(block, 0, width, axis=dim), axis, backward)
        block = jnp.concatenate([low, block, high], axis=dim)
    return block


def block_masks(atom_size, first_block, local_blocks):
    total_blocks = atom_size.shape[0]
    owned = first_block + jnp.arange(local_blocks, dtype=jnp.int32)
    offsets = jnp.arange(W, dtype=jnp.int32)
    partner = owned[:, None] + offsets[None, :] - R
    inside = (partner >= 0) & (partner < total_blocks)
    catalog = jnp.arange(total_blocks, dtype=jnp.int32)
    size_partner = jnp.sum(jnp.where(partner[:, :, None] == catalog, atom_size, 0), axis=2)
    size_owned = jnp.sum(jnp.where(owned[:, None] == catalog, atom_size, 0), axis=1)
    funcs = jnp.arange(BS, dtype=jnp.int32)
    rows_ok = (funcs[None, None, :] < size_partner[:, :, None]) & inside[:, :, None]
    cols_ok = funcs[None, :] < size_owned[:, None]
    pair_ok = rows_ok[:, :, :, None] & cols_ok[:, None, None, :]
    return (inside, pair_ok.reshape(local_blocks, W, BS * BS))


def first_products(padded_occ, tensor):
    rows = tensor.shape[0]
    local_blocks = tensor.shape[1]
    results = []
    for target in range(W):
        total = jnp.zeros((rows, local_blocks, BS, BS), jnp.float32)
        for source in range(W):
            if abs(target - source) <= R:
                green = padded_occ[source : source + local_blocks, target - source + R].reshape(
                    local_blocks, BS, BS
                )
                block = tensor[:, :, source].reshape(rows, local_blocks, BS, BS)
                total = total + jnp.einsum(
                    "nlm,pnmv->pnlv", green, block, preferred_element_type=jnp.float32
                )
        results.append(total.astype(jnp.bfloat16).reshape(rows, local_blocks, BS * BS))
    return jnp.concatenate(results, axis=2).reshape(rows, local_blocks * W * BS * BS)


def second_products(padded_tensor, virt):
    rows = padded_tensor.shape[0]
    local_blocks = virt.shape[0]
    results = []
    for target in range(W):
        total = jnp.zeros((rows, local_blocks, BS, BS), jnp.float32)
        for source in range(W):
            if abs(target - source) <= R:
                block = padded_tensor[
                    :, source : source + local_blocks, target - source + R
                ].reshape(rows, local_blocks, BS, BS)
                green = virt[:, source].reshape(local_blocks, BS, BS)
                total = total + jnp.einsum(
                    "pnls,nsv->pnlv", block, green, preferred_element_type=jnp.float32
                )
        results.append(total.astype(jnp.bfloat16).reshape(rows, local_blocks, BS * BS))
    return jnp.concatenate(results, axis=2).reshape(rows, local_blocks * W * BS * BS)


def body(three_center, atom_size, tensor_pattern, green_occ, green_virt, green_pattern):
    regrouped = lax.all_to_all(three_center, "orb", split_axis=1, concat_axis=0, tiled=True)
    local_blocks = regrouped.shape[1]
    first_block = lax.axis_index("orb") * local_blocks
    inside, pair_ok = block_masks(atom_size, first_block, local_blocks)
    pattern_rows = jnp.repeat(tensor_pattern, ABS, axis=0)
    keep = (pattern_rows[..., None] > 0) & pair_ok[None]
    tensor = jnp.where(keep, regrouped, jnp.zeros((), regrouped.dtype))
    diagonal = jnp.arange(W, dtype=jnp.int32) == R
    green_keep = ((green_pattern > 0) | diagonal[None, :]) & inside
    green_mask = green_keep[..., None] & pair_ok
    occ = jnp.where(green_mask, green_occ, jnp.zeros((), green_occ.dtype))
    virt = jnp.where(green_mask, green_virt, jnp.zeros((), green_virt.dtype))
    padded_occ = padded(occ, (("orb", 0),), R)
    padded_tensor = padded(tensor, (("orb", 1),), R)
    first = first_products(padded_occ, tensor)
    second = second_products(padded_tensor, virt)
    left_all, right_all = (
        lax.all_to_all(first, "aux", split_axis=1, concat_axis=0, tiled=True),
        lax.all_to_all(second, "aux", split_axis=1, concat_axis=0, tiled=True),
    )
    row_sums = lax.psum_scatter(
        lax.dot_general(
            left_all, right_all, (((1,), (1,)), ((), ())), preferred_element_type=jnp.float32
        ),
        "aux",
        scatter_dimension=0,
        tiled=True,
    )
    return lax.psum_scatter(row_sums, "orb", scatter_dimension=0, tiled=True)


def solution(mesh):
    return jax.shard_map(
        body,
        mesh=mesh,
        in_specs=(
            P(("aux", "orb"), None, None, None),
            P(),
            P("aux", "orb", None),
            P("orb", None, None),
            P("orb", None, None),
            P("orb", None),
        ),
        out_specs=P(("aux", "orb"), None),
        check_vma=False,
    )
```

profile of v0, /device:TPU:0, one launch (start us, length us, event | category | flops | bytes accessed | tf_op | source)
XLA Modules:
  0.0 547.4 jit_solution(12280116020150700102)
XLA Ops:
  6.5 6.5 %copy.128 = bf16[20,8,3,4096]{3,0,2,1:T(8,128)(2,1)} copy(bf16[20,8,3,4096]{3,1,2,0:T(8,128)(2,1)} %param.6) | data formatting | bytes 7864320 | tf_op args[0]
  13.1 7.5 %all-to-all-start = ((bf16[20,8,3,4096]{3,0,2,1:T(8,128)(2,1)}), bf16[20,8,3,4096]{3,0,2,1:T(8,128)(2,1)}, u32[]{:S(2)}, u32[]{:S(2)}) async-start(bf16[20,8,3,4096]{3,0,2,1:T(8,128)(2,1)} %copy.128), calls=%async_computation | async-start | bytes 9437184 | tf_op jit(solution)/shard_map/all_to_all | solution.py:80
  21.7 0.6 iota_compare_fusion.1
  22.6 3.9 collective-permute-start
  26.5 1.3 collective-permute-start.1
  28.9 30.9 %collective-permute-done = bf16[1,3,4096]{2,1,0:T(4,128)(2,1)S(1)} collective-permute-done((bf16[1,3,4096]{2,1,0:T(4,128)(2,1)S(1)}, bf16[1,3,4096]{2,1,0:T(4,128)(2,1)S(1)}, u32[]{:S(2)}, u32[]{:S(2)}) %collective-permute-start) | collective-permute-done | bytes 24608 | tf_op jit(solution)/shard_map/ppermute | solution.py:17
  60.3 65.1 %all-to-all-done = bf16[20,8,3,4096]{3,0,2,1:T(8,128)(2,1)} async-done(((bf16[20,8,3,4096]{3,0,2,1:T(8,128)(2,1)}), bf16[20,8,3,4096]{3,0,2,1:T(8,128)(2,1)}, u32[]{:S(2)}, u32[]{:S(2)}) %all-to-all-start) | async-done | bytes 3932192 | tf_op jit(solution)/shard_map/all_to_all | solution.py:80
  125.4 5.1 copy.129
  130.5 6.1 %all_to_all.44 = bf16[160,1,3,4096]{3,0,2,1:T(8,128)(2,1)} reshape(bf16[8,20,1,3,4096]{4,1,0,3,2:T(8,128)(2,1)} %copy.129) | data formatting | bytes 7864320 | tf_op jit(solution)/shard_map/all_to_all | solution.py:80
  136.5 5.5 and_select_fusion
  142.0 3.6 fusion.25
  145.6 5.0 collective-permute-start.2
  150.5 1.7 collective-permute-start.3
  152.3 4.8 reshape.442
  157.1 3.9 reshape.440
  161.0 3.9 reshape.447
  164.8 5.6 %copy.131 = bf16[160,64,64]{0,1,2:T(8,128)(2,1)S(1)} copy(bf16[160,64,64]{2,1,0:T(8,128)(2,1)} %reshape.442) | data formatting | bytes 2621440 | tf_op jit(solution)/shard_map/reshape.26
  170.4 6.7 %copy.130 = bf16[160,64,64]{0,1,2:T(8,128)(2,1)} copy(bf16[160,64,64]{2,1,0:T(8,128)(2,1)} %reshape.440) | data formatting | bytes 2621440 | tf_op jit(solution)/shard_map/reshape.23
  177.1 6.6 %copy.135 = bf16[160,64,64]{0,1,2:T(8,128)(2,1)} copy(bf16[160,64,64]{2,1,0:T(8,128)(2,1)} %reshape.447) | data formatting | bytes 2621440 | tf_op jit(solution)/shard_map/reshape.35
  183.8 0.7 fusion.29
  184.4 0.9 copy-done.3
  185.4 0.7 fusion.28
  186.0 0.9 copy-done.4
  186.9 2.0 fusion.6
  189.0 2.7 fusion.27
  191.7 6.2 %copy.136 = bf16[160,1,64,64]{3,2,0,1:T(8,128)(2,1)} copy(bf16[160,1,64,64]{0,2,3,1:T(8,128)(2,1)} %fusion.6) | data formatting | bytes 2621440 | tf_op jit(solution)/shard_map/convert_element_type | solution.py:56
  198.0 4.7 reshape.449
  202.6 4.8 fusion.7
  207.4 6.4 %copy.132 = bf16[160,1,64,64]{3,2,0,1:T(8,128)(2,1)} copy(bf16[160,1,64,64]{0,2,3,1:T(8,128)(2,1)} %fusion.7) | data formatting | bytes 2621440 | tf_op jit(solution)/shard_map/convert_element_type | solution.py:56
  213.8 4.7 reshape.444
  218.5 0.7 fusion.30
  219.2 0.9 copy-done.5
  220.1 2.1 fusion.8
  222.2 5.3 copy.139
  227.5 2.9 reshape.452
  230.4 3.6 pad_maximum_fusion
  234.0 9.0 %all_to_all.45 = bf16[160,4,3072]{2,1,0:T(4,128)(2,1)} reshape(bf16[160,1,12288]{2,0,1:T(8,128)(2,1)} %pad_maximum_fusion) | data formatting | bytes 7864320 | tf_op jit(solution)/shard_map/all_to_all | solution.py:97
  242.9 5.2 copy.140
  248.1 5.2 all-to-all-start.1
  253.6 4.8 fusion.2
  258.4 4.8 fusion.4
  263.2 4.8 fusion
  268.1 48.6 %collective-permute-done.2 = bf16[160,1,3,4096]{3,0,2,1:T(8,128)(2,1)} collective-permute-done((bf16[160,1,3,4096]{3,0,2,1:T(8,128)(2,1)}, bf16[160,1,3,4096]{3,0,2,1:T(8,128)(2,1)}, u32[]{:S(2)}, u32[]{:S(2)}) %collective-permute-start.2) | collective-permute-done | bytes 3932192 | tf_op jit(solution)/shard_map/ppermute | solution.py:17
  316.6 3.0 fusion.23
  319.7 3.3 copy.145
  323.0 3.6 fusion.24
  326.6 2.7 fusion.17
  329.3 3.1 copy.149
  332.4 5.6 %add_convert_fusion.1 = bf16[64,160,64]{1,0,2:T(8,128)(2,1)} fusion(f32[64,160,64]{1,0,2:T(8,128)} %fusion.17, f32[64,160,64]{1,0,2:T(8,128)} %fusion.2, bf16[160,64,64]{0,2,1:T(8,128)(2,1)S(1)} %bitcast.122, bf16[64,64]{1,0:T(8,128)(2,1)S(1)} %reshape.458), kind=kOutput, calls=%fused_computation.2 | convolution fusion | flops 85852160 | bytes 7872512 | tf_op jit(solution)/shard_map/pnls,nsv->pnlv/dot_general | solution.py:72
  338.0 3.8 copy.156
  341.8 1.8 copy.141
  343.6 4.2 add_convert_fusion.2
  347.9 3.9 copy.155
  351.8 1.8 copy.153
  353.6 4.3 add_convert_fusion
  357.9 4.0 copy.157
  361.9 3.1 pad_maximum_fusion.1
  365.0 9.0 %all_to_all.49 = bf16[160,4,3072]{2,1,0:T(4,128)(2,1)} reshape(bf16[160,1,12288]{2,0,1:T(8,128)(2,1)} %pad_maximum_fusion.1) | data formatting | bytes 7864320 | tf_op jit(solution)/shard_map/all_to_all | solution.py:98
  373.9 5.2 copy.158
  379.1 49.1 %all_to_all.56 = bf16[160,4,3072]{2,0,1:T(8,128)(2,1)S(1)} all-to-all(bf16[160,4,3072]{2,0,1:T(8,128)(2,1)} %copy.158), channel_id=1, replica_groups=mesh['aux'=4,'orb'=8] {'aux'}, dimensions={1} | all-to-all | bytes 7864320 | tf_op jit(solution)/shard_map/all_to_all | solution.py:98
  428.2 6.6 %fusion.26 = f32[640,640]{1,0:T(8,128)} fusion(bf16[640,3072]{1,0:T(8,128)(2,1)} %bitcast.10, bf16[640,3072]{1,0:T(8,128)(2,1)S(1)} %bitcast.128), kind=kOutput, calls=%fused_computation.57 | convolution fusion | flops 2516582400 | bytes 9502720 | tf_op jit(solution)/shard_map/dot_general | solution.py:101
  434.8 28.5 %reduce-scatter.2.cloned.1.call-done = f32[160,640]{1,0:T(8,128)} async-done(((f32[640,640]{1,0:T(8,128)}), f32[160,640]{1,0:T(8,128)}) %reduce-scatter.2.cloned.1.call-update) | async-done | bytes 409616 | tf_op jit(solution)/shard_map/reduce_scatter | solution.py:100
  464.6 74.2 %all-reduce.3.cloned.1.call-done = f32[160,640]{1,0:T(8,128)} async-done(((f32[160,640]{1,0:T(8,128)}), f32[160,640]{1,0:T(8,128)}) %all-reduce.3.cloned.1.call-update) | async-done | bytes 409616
  538.8 1.5 constant_dynamic-slice_fusion
  (65 shorter events, 3.9 us)
Async XLA Ops:
  13.0 7.5 %copy-start.12 = (s32[8]{0:T(128)S(1)}, s32[8]{0:T(128)}, u32[]{:S(2)}) copy-start(s32[8]{0:T(128)} %param.7) | copy-start | bytes 100
  13.0 9.4 %copy-start.13 = (s32[1,3]{1,0:T(1,128)S(1)}, s32[1,3]{1,0:T(1,128)}, u32[]{:S(2)}) copy-start(s32[1,3]{1,0:T(1,128)} %param.11) | copy-start | bytes 40
  13.0 9.4 %copy-start.9 = (bf16[1,3,4096]{2,1,0:T(4,128)(2,1)S(1)}, bf16[1,3,4096]{2,1,0:T(4,128)(2,1)}, u32[]{:S(2)}) copy-start(bf16[1,3,4096]{2,1,0:T(4,128)(2,1)} %param.10) | copy-start | bytes 73732
  13.0 9.4 %copy-start.10 = (bf16[1,3,4096]{2,1,0:T(4,128)(2,1)S(1)}, bf16[1,3,4096]{2,1,0:T(4,128)(2,1)}, u32[]{:S(2)}) copy-start(bf16[1,3,4096]{2,1,0:T(4,128)(2,1)} %param.9) | copy-start | bytes 73732
  13.0 14.9 %copy-start.11 = (s32[10,1,3]{0,1,2:T(1,128)S(1)}, s32[10,1,3]{0,1,2:T(1,128)}, u32[]{:S(2)}) copy-start(s32[10,1,3]{0,1,2:T(1,128)} %param.8) | copy-start | bytes 364
  13.1 112.3 %all-to-all-start = ((bf16[20,8,3,4096]{3,0,2,1:T(8,128)(2,1)}), bf16[20,8,3,4096]{3,0,2,1:T(8,128)(2,1)}, u32[]{:S(2)}, u32[]{:S(2)}) async-start(bf16[20,8,3,4096]{3,0,2,1:T(8,128)(2,1)} %copy.128), calls=%async_computation | async-start | bytes 9437184 | tf_op jit(solution)/shard_map/all_to_all | solution.py:80
  22.6 37.2 %collective-permute-start = (bf16[1,3,4096]{2,1,0:T(4,128)(2,1)S(1)}, bf16[1,3,4096]{2,1,0:T(4,128)(2,1)S(1)}, u32[]{:S(2)}, u32[]{:S(2)}) collective-permute-start(bf16[1,3,4096]{2,1,0:T(4,128)(2,1)S(1)} %get-tuple-element.23), channel_id=1, source_target_pairs={{0,1},{1,2},{2,3},{3,4},{4,5},{5,6},{6,7},{8,9},{9,10},{10,11},{11... | collective-permute-start | bytes 73736 | tf_op jit(solution)/shard_map/ppermute | solution.py:17
  26.5 33.5 %collective-permute-start.1 = (bf16[1,3,4096]{2,1,0:T(4,128)(2,1)S(1)}, bf16[1,3,4096]{2,1,0:T(4,128)(2,1)S(1)}, u32[]{:S(2)}, u32[]{:S(2)}) collective-permute-start(bf16[1,3,4096]{2,1,0:T(4,128)(2,1)S(1)} %get-tuple-element.23), channel_id=1, source_target_pairs={{1,0},{2,1},{3,2},{4,3},{5,4},{6,5},{7,6},{9,8},{10,9},{11,10},{12... | collective-permute-start | bytes 73736 | tf_op jit(solution)/shard_map/ppermute | solution.py:20
  145.6 171.1 %collective-permute-start.2 = (bf16[160,1,3,4096]{3,0,2,1:T(8,128)(2,1)}, bf16[160,1,3,4096]{3,0,2,1:T(8,128)(2,1)}, u32[]{:S(2)}, u32[]{:S(2)}) collective-permute-start(bf16[160,1,3,4096]{3,0,2,1:T(8,128)(2,1)} %and_select_fusion), channel_id=1, source_target_pairs={{0,1},{1,2},{2,3},{3,4},{4,5},{5,6},{6,7},{8,9},{9,10},{10,11},{11... | collective-permute-start | bytes 11796488 | tf_op jit(solution)/shard_map/ppermute | solution.py:17
  150.5 172.5 %collective-permute-start.3 = (bf16[160,1,3,4096]{3,0,2,1:T(8,128)(2,1)}, bf16[160,1,3,4096]{3,0,2,1:T(8,128)(2,1)}, u32[]{:S(2)}, u32[]{:S(2)}) collective-permute-start(bf16[160,1,3,4096]{3,0,2,1:T(8,128)(2,1)} %and_select_fusion), channel_id=1, source_target_pairs={{1,0},{2,1},{3,2},{4,3},{5,4},{6,5},{7,6},{9,8},{10,9},{11,10},{12... | collective-permute-start | bytes 11796488 | tf_op jit(solution)/shard_map/ppermute | solution.py:20
  183.8 1.6 copy-start.3
  185.3 1.6 copy-start.4
  218.5 1.6 copy-start.5
  248.1 5.4 copy-start
  248.1 131.0 %all-to-all-start.1 = ((bf16[160,4,3072]{2,0,1:T(8,128)(2,1)}), bf16[160,4,3072]{2,0,1:T(8,128)(2,1)}, u32[]{:S(2)}, u32[]{:S(2)}) async-start(bf16[160,4,3072]{2,0,1:T(8,128)(2,1)} %copy.140), calls=%async_computation.1 | async-start | bytes 7864320 | tf_op jit(solution)/shard_map/all_to_all | solution.py:97
  253.3 210.0 %reduce-scatter.2.cloned.1.call-start = ((), (), s32[]{:S(2)}) async-start(), calls=%async_computation.4 | async-start | bytes 2048000 | tf_op jit(solution)/shard_map/reduce_scatter | solution.py:100
  253.5 4.9 copy-start.1
  258.4 4.8 copy-start.2
  347.9 3.9 copy-start.6
  357.9 4.0 copy-start.7
  357.9 4.0 copy-start.8
  428.2 35.2 %copy-start.14 = (u32[32]{0:T(128)S(1)}, u32[32]{0:T(128)}, u32[]{:S(2)}) copy-start(u32[32]{0:T(128)} %constant.24) | copy-start | bytes 388
  434.8 104.0 %all-reduce.3.cloned.1.call-start = ((), (), s32[]{:S(2)}) async-start(), calls=%async_computation.5 | async-start | bytes 819200
Sparse Core Ops, SparseCore 0:
  434.9 28.3 reduce-scatter.1
  466.7 72.0 all-reduce.2
where the time goes:
time: 555 us; the launch traced here: 547 us
  waiting for transfers between devices  247 us (45%)
  local copies, waits for them, and re-layouts  146 us (26%)
  matrix products  51.6 us (9%)
  blocking collectives  49.1 us (9%)
  starting transfers between devices  24.8 us (4%)
  between operations  14.6 us (3%)
  other arithmetic  13.9 us (3%)
    ppermute x2, waiting for transfers between devices, padded(): lax.ppermute(lax.slice_in_dim(block, block.shape[dim] - width, None, axis...  79.4 us
    unnamed x3, waiting for transfers between devices  74.2 us
    all_to_all x1, waiting for transfers between devices, body(): lax.all_to_all(three_center, 'orb', split_axis=1, concat_axis=0, tiled=True)  65.1 us
    all_to_all x1, blocking collectives, body(): lax.all_to_all(second, 'aux', split_axis=1, concat_axis=0, tiled=True)  49.1 us
    another operation x16, local copies, waits for them, and re-layouts  32.3 us
    dot_general x7, matrix products, second_products(): jnp.einsum('pnls,nsv->pnlv', block, green, preferred_element_type=jnp.flo...  31.3 us
    reduce_scatter x1, waiting for transfers between devices, body(): lax.psum_scatter(lax.dot_general(left_all, right_all, (((1,), (1,)), ((),...  28.5 us
    convert_element_type x3, local copies, waits for them, and re-layouts, first_products(): total.astype(jnp.bfloat16).reshape(rows, local_blocks, BS * BS)  17.9 us
  transfers between devices with their start and end apart: 8, of which 5 were waited for; matrix products, arithmetic and copies ran while one was open for 29% of the time, Pallas kernels for 0%

commit v1 on v0

--- a/solution.py
+++ b/solution.py
@@ -77,7 +77,12 @@
 
 
 def body(three_center, atom_size, tensor_pattern, green_occ, green_virt, green_pattern):
-    regrouped = lax.all_to_all(three_center, "orb", split_axis=1, concat_axis=0, tiled=True)
+    regrouped = jnp.concatenate(
+        lax.all_to_all(
+            jnp.stack(jnp.split(three_center, lax.axis_size("orb"), axis=1)), "orb", 0, 0
+        ),
+        axis=0,
+    )
     local_blocks = regrouped.shape[1]
     first_block = lax.axis_index("orb") * local_blocks
     inside, pair_ok = block_masks(atom_size, first_block, local_blocks)

time: 555 us -> 581 us (1.047)
  local copies, waits for them, and re-layouts: 146 us -> 167 us
    split x0 -> x1, local copies, waits for them, and re-layouts: none -> 18.3 us  [body(): jnp.split(three_center, lax.axis_size('orb'), axis=1)]
    reshape x0 -> x1, local copies, waits for them, and re-layouts: none -> 6.07 us  [body(): jnp.concatenate(lax.all_to_all(jnp.stack(jnp.split(three_center, lax.axis...]
    all_to_all x2 -> x1, local copies, waits for them, and re-layouts: 11.1 us -> 5.14 us  [body(): lax.all_to_all(jnp.stack(jnp.split(three_center, lax.axis_size('orb'), ax...]
    another operation x16 -> x17, local copies, waits for them, and re-layouts: 32.3 us -> 34.2 us
    unnamed x34 -> x40, local copies, waits for them, and re-layouts: 11.4 us -> 12.6 us
  transfers between devices with their start and end apart: 8 -> 8, of which waited for: 5 -> 5; matrix products, arithmetic and copies ran while one was open for 29% -> 28% of each run, Pallas kernels for 0% -> 0%
where the time goes in v1:
time: 581 us; the launch traced here: 570 us
  waiting for transfers between devices  246 us (42%)
  local copies, waits for them, and re-layouts  167 us (29%)
  matrix products  54.6 us (9%)
  blocking collectives  49.1 us (8%)
  starting transfers between devices  24.7 us (4%)
  between operations  14.6 us (3%)
  other arithmetic  13.8 us (2%)
    ppermute x2, waiting for transfers between devices, padded(): lax.ppermute(lax.slice_in_dim(block, block.shape[dim] - width, None, axis...  78.6 us
    unnamed x3, waiting for transfers between devices  74.2 us
    all_to_all x1, waiting for transfers between devices, body(): lax.all_to_all(jnp.stack(jnp.split(three_center, lax.axis_size('orb'), ax...  64.5 us
    all_to_all x1, blocking collectives, body(): lax.all_to_all(second, 'aux', split_axis=1, concat_axis=0, tiled=True)  49.1 us
    another operation x16, local copies, waits for them, and re-layouts  32.8 us
    dot_general x7, matrix products, second_products(): jnp.einsum('pnls,nsv->pnlv', block, green, preferred_element_type=jnp.flo...  31.2 us
    reduce_scatter x1, waiting for transfers between devices, body(): lax.psum_scatter(lax.dot_general(left_all, right_all, (((1,), (1,)), ((),...  29.1 us
    split x1, local copies, waits for them, and re-layouts, body(): jnp.split(three_center, lax.axis_size('orb'), axis=1)  18.3 us
  transfers between devices with their start and end apart: 8, of which 5 were waited for; matrix products, arithmetic and copies ran while one was open for 28% of the time, Pallas kernels for 0%

profile of v1, /device:TPU:0, one launch (start us, length us, event | category | flops | bytes accessed | tf_op | source)
XLA Modules:
  0.0 570.3 jit_solution(8787560449829070392)
XLA Ops:
  6.5 18.3 %fusion.34 = (bf16[20,1,3,4096]{3,1,2,0:T(2,128)(2,1)S(1)}, bf16[20,1,3,4096]{3,1,2,0:T(2,128)(2,1)S(1)}, bf16[20,1,3,4096]{3,1,2,0:T(2,128)(2,1)S(1)}, bf16[20,...) fusion(bf16[20,8,3,4096]{3,1,2,0:T(8,128)(2,1)} %param.6), kind=kLoop, calls=%fused_computation.73 | loop fusion | bytes 7864320 | tf_op jit(solution)/shard_map/split | solution.py:82
  26.2 1.4 fusion.15
  27.5 1.4 fusion.14
  28.9 1.4 fusion.13
  30.3 1.4 fusion.12
  31.6 1.4 fusion.11
  33.0 1.4 fusion.10
  34.4 1.4 fusion.9
  35.7 7.5 %all-to-all-start = ((bf16[8,20,1,3,4096]{4,1,3,2,0:T(8,128)(2,1)}), bf16[8,20,1,3,4096]{4,1,3,2,0:T(8,128)(2,1)}, u32[]{:S(2)}, u32[]{:S(2)}) async-start(bf16[8,20,1,3,4096]{4,1,3,2,0:T(8,128)(2,1)} %fusion.9), calls=%async_computation | async-start | bytes 9437184 | tf_op jit(solution)/shard_map/all_to_all | solution.py:81
  45.3 3.9 collective-permute-start
  51.6 30.9 %collective-permute-done = bf16[1,3,4096]{2,1,0:T(4,128)(2,1)S(1)} collective-permute-done((bf16[1,3,4096]{2,1,0:T(4,128)(2,1)S(1)}, bf16[1,3,4096]{2,1,0:T(4,128)(2,1)S(1)}, u32[]{:S(2)}, u32[]{:S(2)}) %collective-permute-start) | collective-permute-done | bytes 24608 | tf_op jit(solution)/shard_map/ppermute | solution.py:17
  83.6 64.5 %all-to-all-done = bf16[8,20,1,3,4096]{4,1,3,2,0:T(8,128)(2,1)} async-done(((bf16[8,20,1,3,4096]{4,1,3,2,0:T(8,128)(2,1)}), bf16[8,20,1,3,4096]{4,1,3,2,0:T(8,128)(2,1)}, u32[]{:S(2)}, u32[]{:S(2)}) %all-to-all-start) | async-done | bytes 3932192 | tf_op jit(solution)/shard_map/all_to_all | solution.py:81
  148.1 5.1 copy.135
  153.2 6.1 %reshape.443 = bf16[160,1,3,4096]{3,0,2,1:T(8,128)(2,1)} reshape(bf16[8,20,1,3,4096]{4,1,0,3,2:T(8,128)(2,1)} %copy.135) | data formatting | bytes 7864320 | tf_op jit(solution)/shard_map/reshape | solution.py:80
  159.3 5.5 and_select_fusion
  164.7 3.5 fusion.33
  168.3 5.0 collective-permute-start.2
  173.3 1.5 collective-permute-start.3
  174.7 4.8 reshape.446
  179.5 3.9 reshape.444
  183.4 5.6 copy.137
  189.0 6.6 %copy.136 = bf16[160,64,64]{0,1,2:T(8,128)(2,1)} copy(bf16[160,64,64]{2,1,0:T(8,128)(2,1)} %reshape.444) | data formatting | bytes 2621440 | tf_op jit(solution)/shard_map/reshape.24
  196.4 2.6 fusion.38
  199.0 2.7 fusion.37
  201.7 2.0 fusion.7
  203.8 3.9 reshape.451
  207.6 6.2 %copy.138 = bf16[160,1,64,64]{3,2,0,1:T(8,128)(2,1)} copy(bf16[160,1,64,64]{0,2,3,1:T(8,128)(2,1)} %fusion.7) | data formatting | bytes 2621440 | tf_op jit(solution)/shard_map/convert_element_type | solution.py:56
  213.9 4.6 reshape.448
  218.5 6.6 %copy.141 = bf16[160,64,64]{0,1,2:T(8,128)(2,1)} copy(bf16[160,64,64]{2,1,0:T(8,128)(2,1)} %reshape.451) | data formatting | bytes 2621440 | tf_op jit(solution)/shard_map/reshape.36
  225.1 6.1 %fusion.6 = bf16[160,1,64,64]{0,2,3,1:T(8,128)(2,1)} fusion(f32[160,64,64]{0,2,1:T(8,128)} %fusion.37, f32[160,64,64]{0,2,1:T(8,128)} %fusion.38, bf16[64,64,1]{1,0,2:T(8,128)(2,1)S(1)} %reshape.471, bf16[160,64,64]{0,1,2:T(8,128)(2,1)} %copy.141), kind=kOutput, calls=%fused_computation.15 | convolution fusion | flops 85852160 | bytes 7872512 | tf_op jit(solution)/shard_map/nlm,pnmv->pnlv/dot_general | solution.py:53
  231.2 6.4 %copy.142 = bf16[160,1,64,64]{3,2,0,1:T(8,128)(2,1)} copy(bf16[160,1,64,64]{0,2,3,1:T(8,128)(2,1)} %fusion.6) | data formatting | bytes 2621440 | tf_op jit(solution)/shard_map/convert_element_type | solution.py:56
  237.6 4.6 reshape.453
  243.8 2.0 fusion.8
  245.8 5.3 copy.145
  251.2 2.9 reshape.456
  254.0 3.5 pad_maximum_fusion
  257.5 9.0 %all_to_all.32 = bf16[160,4,3072]{2,1,0:T(4,128)(2,1)} reshape(bf16[160,1,12288]{2,0,1:T(8,128)(2,1)} %pad_maximum_fusion) | data formatting | bytes 7864320 | tf_op jit(solution)/shard_map/all_to_all | solution.py:102
  266.5 5.2 copy.146
  271.6 5.1 all-to-all-start.1
  277.2 4.7 fusion.2
  282.0 4.8 fusion.4
  286.8 4.8 fusion
  291.6 47.7 %collective-permute-done.2 = bf16[160,1,3,4096]{3,0,2,1:T(8,128)(2,1)} collective-permute-done((bf16[160,1,3,4096]{3,0,2,1:T(8,128)(2,1)}, bf16[160,1,3,4096]{3,0,2,1:T(8,128)(2,1)}, u32[]{:S(2)}, u32[]{:S(2)}) %collective-permute-start.2) | collective-permute-done | bytes 3932192 | tf_op jit(solution)/shard_map/ppermute | solution.py:17
  339.3 3.0 fusion.31
  342.3 3.2 copy.151
  345.6 3.5 fusion.32
  349.1 2.7 fusion.25
  351.7 3.1 copy.155
  354.8 5.5 add_convert_fusion.1
  360.4 3.8 copy.162
  364.2 1.8 copy.147
  366.0 4.3 add_convert_fusion.2
  370.4 3.8 copy.161
  374.2 1.8 copy.159
  376.0 4.3 add_convert_fusion
  380.4 3.9 copy.163
  384.3 3.1 pad_maximum_fusion.1
  387.4 9.0 %all_to_all.36 = bf16[160,4,3072]{2,1,0:T(4,128)(2,1)} reshape(bf16[160,1,12288]{2,0,1:T(8,128)(2,1)} %pad_maximum_fusion.1) | data formatting | bytes 7864320 | tf_op jit(solution)/shard_map/all_to_all | solution.py:103
  396.3 5.2 copy.164
  401.5 49.1 %all_to_all.43 = bf16[160,4,3072]{2,0,1:T(8,128)(2,1)S(1)} all-to-all(bf16[160,4,3072]{2,0,1:T(8,128)(2,1)} %copy.164), channel_id=1, replica_groups=mesh['aux'=4,'orb'=8] {'aux'}, dimensions={1} | all-to-all | bytes 7864320 | tf_op jit(solution)/shard_map/all_to_all | solution.py:103
  450.6 6.6 %fusion.35 = f32[640,640]{1,0:T(8,128)} fusion(bf16[640,3072]{1,0:T(8,128)(2,1)} %bitcast.16, bf16[640,3072]{1,0:T(8,128)(2,1)S(1)} %bitcast.157), kind=kOutput, calls=%fused_computation.74 | convolution fusion | flops 2516582400 | bytes 9502720 | tf_op jit(solution)/shard_map/dot_general | solution.py:106
  457.2 29.1 %reduce-scatter.2.cloned.1.call-done = f32[160,640]{1,0:T(8,128)} async-done(((f32[640,640]{1,0:T(8,128)}), f32[160,640]{1,0:T(8,128)}) %reduce-scatter.2.cloned.1.call-update) | async-done | bytes 409616 | tf_op jit(solution)/shard_map/reduce_scatter | solution.py:105
  487.6 74.2 %all-reduce.3.cloned.1.call-done = f32[160,640]{1,0:T(8,128)} async-done(((f32[160,640]{1,0:T(8,128)}), f32[160,640]{1,0:T(8,128)}) %all-reduce.3.cloned.1.call-update) | async-done | bytes 409616
  561.8 1.5 constant_dynamic-slice_fusion
  (73 shorter events, 10.3 us)
Async XLA Ops:
  35.7 7.5 %copy-start.12 = (s32[8]{0:T(128)S(1)}, s32[8]{0:T(128)}, u32[]{:S(2)}) copy-start(s32[8]{0:T(128)} %param.7) | copy-start | bytes 100
  35.7 9.4 %copy-start.13 = (s32[1,3]{1,0:T(1,128)S(1)}, s32[1,3]{1,0:T(1,128)}, u32[]{:S(2)}) copy-start(s32[1,3]{1,0:T(1,128)} %param.11) | copy-start | bytes 40
  35.7 9.4 %copy-start.9 = (bf16[1,3,4096]{2,1,0:T(4,128)(2,1)S(1)}, bf16[1,3,4096]{2,1,0:T(4,128)(2,1)}, u32[]{:S(2)}) copy-start(bf16[1,3,4096]{2,1,0:T(4,128)(2,1)} %param.10) | copy-start | bytes 73732
  35.7 9.4 %copy-start.10 = (bf16[1,3,4096]{2,1,0:T(4,128)(2,1)S(1)}, bf16[1,3,4096]{2,1,0:T(4,128)(2,1)}, u32[]{:S(2)}) copy-start(bf16[1,3,4096]{2,1,0:T(4,128)(2,1)} %param.9) | copy-start | bytes 73732
  35.7 14.9 %copy-start.11 = (s32[10,1,3]{0,1,2:T(1,128)S(1)}, s32[10,1,3]{0,1,2:T(1,128)}, u32[]{:S(2)}) copy-start(s32[10,1,3]{0,1,2:T(1,128)} %param.8) | copy-start | bytes 364
  35.7 112.3 %all-to-all-start = ((bf16[8,20,1,3,4096]{4,1,3,2,0:T(8,128)(2,1)}), bf16[8,20,1,3,4096]{4,1,3,2,0:T(8,128)(2,1)}, u32[]{:S(2)}, u32[]{:S(2)}) async-start(bf16[8,20,1,3,4096]{4,1,3,2,0:T(8,128)(2,1)} %fusion.9), calls=%async_computation | async-start | bytes 9437184 | tf_op jit(solution)/shard_map/all_to_all | solution.py:81
  45.3 37.2 %collective-permute-start = (bf16[1,3,4096]{2,1,0:T(4,128)(2,1)S(1)}, bf16[1,3,4096]{2,1,0:T(4,128)(2,1)S(1)}, u32[]{:S(2)}, u32[]{:S(2)}) collective-permute-start(bf16[1,3,4096]{2,1,0:T(4,128)(2,1)S(1)} %get-tuple-element.31), channel_id=1, source_target_pairs={{0,1},{1,2},{2,3},{3,4},{4,5},{5,6},{6,7},{8,9},{9,10},{10,11},{11... | collective-permute-start | bytes 73736 | tf_op jit(solution)/shard_map/ppermute | solution.py:17
  49.2 34.1 %collective-permute-start.1 = (bf16[1,3,4096]{2,1,0:T(4,128)(2,1)S(1)}, bf16[1,3,4096]{2,1,0:T(4,128)(2,1)S(1)}, u32[]{:S(2)}, u32[]{:S(2)}) collective-permute-start(bf16[1,3,4096]{2,1,0:T(4,128)(2,1)S(1)} %get-tuple-element.31), channel_id=1, source_target_pairs={{1,0},{2,1},{3,2},{4,3},{5,4},{6,5},{7,6},{9,8},{10,9},{11,10},{12... | collective-permute-start | bytes 73736 | tf_op jit(solution)/shard_map/ppermute | solution.py:20
  168.3 171.1 %collective-permute-start.2 = (bf16[160,1,3,4096]{3,0,2,1:T(8,128)(2,1)}, bf16[160,1,3,4096]{3,0,2,1:T(8,128)(2,1)}, u32[]{:S(2)}, u32[]{:S(2)}) collective-permute-start(bf16[160,1,3,4096]{3,0,2,1:T(8,128)(2,1)} %and_select_fusion), channel_id=1, source_target_pairs={{0,1},{1,2},{2,3},{3,4},{4,5},{5,6},{6,7},{8,9},{9,10},{10,11},{11... | collective-permute-start | bytes 11796488 | tf_op jit(solution)/shard_map/ppermute | solution.py:17
  173.3 172.3 %collective-permute-start.3 = (bf16[160,1,3,4096]{3,0,2,1:T(8,128)(2,1)}, bf16[160,1,3,4096]{3,0,2,1:T(8,128)(2,1)}, u32[]{:S(2)}, u32[]{:S(2)}) collective-permute-start(bf16[160,1,3,4096]{3,0,2,1:T(8,128)(2,1)} %and_select_fusion), channel_id=1, source_target_pairs={{1,0},{2,1},{3,2},{4,3},{5,4},{6,5},{7,6},{9,8},{10,9},{11,10},{12... | collective-permute-start | bytes 11796488 | tf_op jit(solution)/shard_map/ppermute | solution.py:20
  196.3 2.7 copy-start.3
  196.3 2.6 copy-start.8
  242.2 1.6 copy-start.4
  271.6 5.5 copy-start
  271.6 129.9 %all-to-all-start.1 = ((bf16[160,4,3072]{2,0,1:T(8,128)(2,1)}), bf16[160,4,3072]{2,0,1:T(8,128)(2,1)}, u32[]{:S(2)}, u32[]{:S(2)}) async-start(bf16[160,4,3072]{2,0,1:T(8,128)(2,1)} %copy.146), calls=%async_computation.1 | async-start | bytes 7864320 | tf_op jit(solution)/shard_map/all_to_all | solution.py:102
  276.7 209.6 %reduce-scatter.2.cloned.1.call-start = ((), (), s32[]{:S(2)}) async-start(), calls=%async_computation.4 | async-start | bytes 2048000 | tf_op jit(solution)/shard_map/reduce_scatter | solution.py:105
  277.2 4.7 copy-start.1
  282.0 4.8 copy-start.2
  366.0 8.1 %copy-start.5 = (bf16[160,1,1,4096]{3,0,2,1:T(8,128)(2,1)S(1)}, bf16[160,1,1,4096]{3,0,2,1:T(8,128)(2,1)}, u32[]{:S(2)}) copy-start(bf16[160,1,1,4096]{3,0,2,1:T(8,128)(2,1)} %get-tuple-element.18) | copy-start | bytes 3932164
  376.0 8.3 %copy-start.6 = (bf16[160,1,4096]{2,0,1:T(8,128)(2,1)S(1)}, bf16[160,1,4096]{2,0,1:T(8,128)(2,1)}, u32[]{:S(2)}) copy-start(bf16[160,1,4096]{2,0,1:T(8,128)(2,1)} %copy.162) | copy-start | bytes 3932164
  380.4 3.9 copy-start.7
  450.6 35.8 %copy-start.14 = (u32[32]{0:T(128)S(1)}, u32[32]{0:T(128)}, u32[]{:S(2)}) copy-start(u32[32]{0:T(128)} %constant.24) | copy-start | bytes 388
  457.2 104.6 %all-reduce.3.cloned.1.call-start = ((), (), s32[]{:S(2)}) async-start(), calls=%async_computation.5 | async-start | bytes 819200
Sparse Core Ops, SparseCore 0:
  457.3 28.9 reduce-scatter.1
  489.7 71.9 all-reduce.2
